TPU v7x, 512 devices: a whole 4x8x8 slice. The times are simulated.
512 devices in a mesh: rep: 8 (over z_hi, core), fsdp: 64 (over y, x, z_lo).
Axes of the slice: x: 4, y: 8, z: 8 (z_hi: 4, z_lo: 2; z = z_hi * 2 + z_lo), core: 2. Of those that a mesh axis runs over, the one named last changes fastest.
Arguments:
- acts: bfloat16 [8, 8192, 8192], P('rep', 'fsdp'), may hold values from -16 to 16
- value_cots: bfloat16 [8, 8192, 512], P('rep', 'fsdp'), may hold values from -0.059814453 to 0.059814453
- inner_weights: float32 [8, 8192, 512], P('rep', 'fsdp'), may hold values from -0.0625 to 0.0625
- first_moment: float32 [8, 8192, 512], P('rep', 'fsdp'), may hold values from -1.8 to 1.8
- second_moment: float32 [8, 8192, 512], P('rep', 'fsdp'), may hold values from 0.01 to 1
- anchor: float32 [8192, 512], P('fsdp'), may hold values from -0.0625 to 0.0625
- outer_momentum: float32 [8192, 512], P('fsdp'), may hold values from -0.06 to 0.06
Outputs:
- first_next: float32 [8, 8192, 512], P('rep', 'fsdp')
- values_next: bfloat16 [8, 8192, 512], P('rep', 'fsdp')
All inputs are finite; a program needn't handle non-finite values.
Results may differ from a plain program's by a relative error of at most 0.0049.
Values may be sent and summed in bfloat16 or wider, within the bound.
A program may use at most 64 MiB of HBM per device.

v0:
```python
import jax
import jax.numpy as jnp
from jax import lax
from jax.sharding import PartitionSpec as P

decay_first = 0.9
decay_second = 0.95
inner_rate = 0.006
epsilon = 1e-08
outer_rate = 0.7
outer_decay = 0.9


def outer_update(average, anchor_rows, momentum_rows):
    velocity = outer_decay * momentum_rows + average
    return (anchor_rows - outer_rate * (average + outer_decay * velocity)).astype(jnp.bfloat16)


def on_device(acts, value_cots, inner_weights, first_moment, second_moment, anchor, outer_momentum):
    tokens_local = acts[0]
    cots_local = value_cots[0]
    rep_count = lax.axis_size("rep")
    feature_split = lax.all_to_all(tokens_local, "fsdp", split_axis=1, concat_axis=0, tiled=True)
    columns = feature_split
    gradient = lax.dot_general(
        columns,
        lax.all_gather(cots_local, "fsdp", axis=0, tiled=True),
        (((0,), (0,)), ((), ())),
        preferred_element_type=jnp.float32,
    )
    first_next = decay_first * first_moment[0] + (1.0 - decay_first) * gradient
    second_next = decay_second * second_moment[0] + (1.0 - decay_second) * gradient * gradient
    stepped = inner_weights[0] - inner_rate * first_next / (jnp.sqrt(second_next) + epsilon)
    drift = anchor - stepped
    summed_drift = lax.psum(drift, "rep")
    weights_next = outer_update(summed_drift / rep_count, anchor, outer_momentum)
    columns = tokens_local
    values = jnp.dot(
        columns,
        lax.all_gather(weights_next, "fsdp", axis=0, tiled=True),
        preferred_element_type=jnp.float32,
    )
    return (first_next[None], values.astype(jnp.bfloat16)[None])


def solution(mesh):
    placed = (
        P("rep", "fsdp", None),
        P("rep", "fsdp", None),
        P("rep", "fsdp", None),
        P("rep", "fsdp", None),
        P("rep", "fsdp", None),
        P("fsdp", None),
        P("fsdp", None),
    )
    return jax.shard_map(
        on_device,
        mesh=mesh,
        in_specs=placed,
        out_specs=(P("rep", "fsdp", None), P("rep", "fsdp", None)),
        check_vma=False,
    )
```

profile of v0, /device:TPU:2, one launch (start us, length us, event | category | flops | bytes accessed | tf_op | source)
XLA Modules:
  0.0 755.7 jit_solution(2856607011129081235)
XLA Ops:
  7.2 0.0 all-gather.6.cloned.1.call-start
  7.2 0.7 all-gather.6.cloned.1.call-update
  7.9 0.0 all-reduce.2.cloned.1.call-start
  7.9 3.2 copy.11
  11.2 74.7 %all_to_all.19 = bf16[128,64,128]{0,2,1:T(8,128)(2,1)} all-to-all(bf16[128,64,128]{0,2,1:T(8,128)(2,1)S(1)} %bitcast.35), channel_id=1, replica_groups=mesh['rep'=8,'fsdp'=64] {'fsdp'}, dimensions={1} | all-to-all | bytes 4194304 | tf_op jit(solution)/shard_map/all_to_all | solution.py:23
  85.9 0.0 copy-start
  85.9 0.0 copy-start.1
  85.9 0.0 copy-start.2
  85.9 0.0 copy-start.3
  85.9 3.3 copy.12
  89.2 248.0 %all-gather.6.cloned.1.call-done = bf16[1,8192,512]{2,1,0:T(8,128)(2,1)} async-done(((bf16[1,128,512]{2,1,0:T(8,128)(2,1)}), bf16[1,8192,512]{2,1,0:T(8,128)(2,1)}) %all-gather.6.cloned.1.call-update) | async-done | bytes 8388624 | tf_op jit(solution)/shard_map/all_gather | solution.py:27
  337.2 0.0 copy-done
  337.2 0.0 copy-done.1
  337.2 0.0 copy-done.2
  337.2 0.0 copy-done.3
  337.2 0.0 copy-start.4
  337.2 5.7 fusion.15
  342.9 0.0 all-reduce.2.cloned.1.call-update
  342.9 0.0 all-gather.4.cloned.1.call-start
  343.0 82.9 %all-reduce.2.cloned.1.call-done = f32[128,512]{1,0:T(8,128)} async-done(((f32[128,512]{1,0:T(8,128)}), f32[128,512]{1,0:T(8,128)}) %all-reduce.2.cloned.1.call-update) | async-done | bytes 262160 | tf_op jit(solution)/shard_map/psum | solution.py:35
  425.8 0.0 copy-done.4
  425.8 1.7 subtract_convert_fusion
  427.5 0.0 all-gather.4.cloned.1.call-update
  427.6 314.5 %all-gather.4.cloned.1.call-done = bf16[8192,512]{1,0:T(8,128)(2,1)} async-done(((bf16[128,512]{1,0:T(8,128)(2,1)}), bf16[8192,512]{1,0:T(8,128)(2,1)}) %all-gather.4.cloned.1.call-update) | async-done | bytes 8388624 | tf_op jit(solution)/shard_map/all_gather | solution.py:40
  742.1 6.4 fusion.7
  748.4 0.8 copy.13
Async XLA Ops:
  7.2 330.1 %all-gather.6.cloned.1.call-start = ((), (), s32[]{:S(2)}) async-start(), calls=%async_computation.3 | async-start | bytes 8519680 | tf_op jit(solution)/shard_map/all_gather | solution.py:27
  7.9 417.9 %all-reduce.2.cloned.1.call-start = ((), (), s32[]{:S(2)}) async-start(), calls=%async_computation.1 | async-start | bytes 524288 | tf_op jit(solution)/shard_map/psum | solution.py:35
  85.9 251.4 %copy-start = (f32[128,512]{1,0:T(8,128)S(1)}, f32[128,512]{1,0:T(8,128)}, u32[]{:S(2)}) copy-start(f32[128,512]{1,0:T(8,128)} %param.12) | copy-start | bytes 786436
  85.9 251.4 %copy-start.1 = (f32[1,128,512]{2,1,0:T(8,128)S(1)}, f32[1,128,512]{2,1,0:T(8,128)}, u32[]{:S(2)}) copy-start(f32[1,128,512]{2,1,0:T(8,128)} %param.9) | copy-start | bytes 786436
  85.9 251.4 %copy-start.2 = (f32[1,128,512]{2,1,0:T(8,128)S(1)}, f32[1,128,512]{2,1,0:T(8,128)}, u32[]{:S(2)}) copy-start(f32[1,128,512]{2,1,0:T(8,128)} %param.11) | copy-start | bytes 786436
  85.9 251.4 %copy-start.3 = (f32[1,128,512]{2,1,0:T(8,128)S(1)}, f32[1,128,512]{2,1,0:T(8,128)}, u32[]{:S(2)}) copy-start(f32[1,128,512]{2,1,0:T(8,128)} %param.10) | copy-start | bytes 786436
  337.2 88.6 %copy-start.4 = (f32[128,512]{1,0:T(8,128)S(1)}, f32[128,512]{1,0:T(8,128)}, u32[]{:S(2)}) copy-start(f32[128,512]{1,0:T(8,128)} %param.13) | copy-start | bytes 786436
  342.9 399.1 %all-gather.4.cloned.1.call-start = ((), (), s32[]{:S(2)}) async-start(), calls=%async_computation.2 | async-start | bytes 8519680 | tf_op jit(solution)/shard_map/all_gather | solution.py:40
Sparse Core Ops, SparseCore 0:
  10.1 327.0 all-gather.5
  343.1 82.7 all-reduce.1
  428.7 313.3 all-gather.3
where the time goes:
time: 756 us
  waiting for transfers between devices  646 us (85%)
  blocking collectives  74.7 us (10%)
  between operations  13.8 us (2%)
  matrix products  12 us (2%)
    all_gather x1, waiting for transfers between devices, on_device(): lax.all_gather(weights_next, 'fsdp', axis=0, tiled=True)  315 us
    all_gather x1, waiting for transfers between devices, on_device(): lax.all_gather(cots_local, 'fsdp', axis=0, tiled=True)  248 us
    psum x1, waiting for transfers between devices, on_device(): summed_drift = lax.psum(drift, 'rep')  82.9 us
    all_to_all x1, blocking collectives, on_device(): lax.all_to_all(tokens_local, 'fsdp', split_axis=1, concat_axis=0, tiled=T...  74.7 us
  transfers between devices with their start and end apart: 3, of which 3 were waited for; matrix products, arithmetic and copies ran while one was open for 1% of the time, Pallas kernels for 0%

commit v1 on v0

--- a/solution.py
+++ b/solution.py
@@ -9,6 +9,11 @@
 epsilon = 1e-08
 outer_rate = 0.7
 outer_decay = 0.9
+
+
+def gather_and_add(shard, mesh_axis):
+    shards = lax.all_gather(shard, mesh_axis)
+    return jnp.sum(shards, axis=0)
 
 
 def outer_update(average, anchor_rows, momentum_rows):
@@ -32,7 +37,7 @@
     second_next = decay_second * second_moment[0] + (1.0 - decay_second) * gradient * gradient
     stepped = inner_weights[0] - inner_rate * first_next / (jnp.sqrt(second_next) + epsilon)
     drift = anchor - stepped
-    summed_drift = lax.psum(drift, "rep")
+    summed_drift = gather_and_add(drift, "rep")
     weights_next = outer_update(summed_drift / rep_count, anchor, outer_momentum)
     columns = tokens_local
     values = jnp.dot(

time: 756 us -> 716 us (0.947)
  waiting for transfers between devices: 646 us -> 606 us
    psum x1 -> x0, waiting for transfers between devices: 82.9 us -> none  [on_device(): summed_drift = lax.psum(drift, 'rep')]
    all_gather x0 -> x1, waiting for transfers between devices: none -> 42.1 us  [gather_and_add(): shards = lax.all_gather(shard, mesh_axis)]
where the time goes in v1:
time: 716 us
  waiting for transfers between devices  606 us (85%)
  blocking collectives  74.7 us (10%)
  between operations  13.8 us (2%)
  matrix products  11.4 us (2%)
  local copies, waits for them, and re-layouts  7.33 us (1%)
    all_gather x1, waiting for transfers between devices, on_device(): lax.all_gather(weights_next, 'fsdp', axis=0, tiled=True)  315 us
    all_gather x1, waiting for transfers between devices, on_device(): lax.all_gather(cots_local, 'fsdp', axis=0, tiled=True)  248 us
    all_to_all x1, blocking collectives, on_device(): lax.all_to_all(tokens_local, 'fsdp', split_axis=1, concat_axis=0, tiled=T...  74.7 us
    all_gather x1, waiting for transfers between devices, gather_and_add(): shards = lax.all_gather(shard, mesh_axis)  42.1 us
  transfers between devices with their start and end apart: 3, of which 3 were waited for; matrix products, arithmetic and copies ran while one was open for 1% of the time, Pallas kernels for 0%

profile of v1, /device:TPU:2, one launch (start us, length us, event | category | flops | bytes accessed | tf_op | source)
XLA Modules:
  0.0 716.0 jit_solution(6697084526782444693)
XLA Ops:
  7.2 0.0 all-gather.8.cloned.1.call-start
  7.2 0.7 all-gather.8.cloned.1.call-update
  7.9 0.0 all-gather.10.cloned.1.call-start
  7.9 3.2 copy.11
  11.2 74.7 %all_to_all.19 = bf16[128,64,128]{0,2,1:T(8,128)(2,1)} all-to-all(bf16[128,64,128]{0,2,1:T(8,128)(2,1)S(1)} %bitcast.36), channel_id=1, replica_groups=mesh['rep'=8,'fsdp'=64] {'fsdp'}, dimensions={1} | all-to-all | bytes 4194304 | tf_op jit(solution)/shard_map/all_to_all | solution.py:28
  85.9 0.0 copy-start.1
  85.9 0.0 copy-start.2
  85.9 0.0 copy-start.3
  85.9 0.0 copy-start.4
  85.9 3.3 copy.12
  89.2 248.0 %all-gather.8.cloned.1.call-done = bf16[1,8192,512]{2,1,0:T(8,128)(2,1)} async-done(((bf16[1,128,512]{2,1,0:T(8,128)(2,1)}), bf16[1,8192,512]{2,1,0:T(8,128)(2,1)}) %all-gather.8.cloned.1.call-update) | async-done | bytes 8388624 | tf_op jit(solution)/shard_map/all_gather | solution.py:32
  337.2 0.0 copy-done.1
  337.2 0.0 copy-done.2
  337.2 0.0 copy-done.3
  337.2 0.0 copy-done.4
  337.2 5.6 fusion.15
  342.9 0.0 copy-start.5
  342.9 0.0 copy-start
  342.9 0.0 all-gather.10.cloned.1.call-update
  342.9 0.0 all-gather.6.cloned.1.call-start
  342.9 42.1 %all-gather.10.cloned.1.call-done = f32[1024,512]{1,0:T(8,128)} async-done(((f32[128,512]{1,0:T(8,128)}), f32[1024,512]{1,0:T(8,128)}) %all-gather.10.cloned.1.call-update) | async-done | bytes 2097168 | tf_op jit(solution)/shard_map/all_gather | solution.py:15
  385.0 1.8 reduce_sum.9
  386.9 0.0 copy-done.5
  386.9 0.7 subtract_convert_fusion
  387.6 0.0 all-gather.6.cloned.1.call-update
  387.6 315.3 %all-gather.6.cloned.1.call-done = bf16[8192,512]{1,0:T(8,128)(2,1)} async-done(((bf16[128,512]{1,0:T(8,128)(2,1)}), bf16[8192,512]{1,0:T(8,128)(2,1)}) %all-gather.6.cloned.1.call-update) | async-done | bytes 8388624 | tf_op jit(solution)/shard_map/all_gather | solution.py:45
  702.9 0.0 copy-done
  702.9 5.8 fusion.7
  708.7 0.8 copy.13
Async XLA Ops:
  7.2 330.1 %all-gather.8.cloned.1.call-start = ((), (), s32[]{:S(2)}) async-start(), calls=%async_computation.2 | async-start | bytes 8519680 | tf_op jit(solution)/shard_map/all_gather | solution.py:32
  7.9 377.1 %all-gather.10.cloned.1.call-start = ((), (), s32[]{:S(2)}) async-start(), calls=%async_computation.3 | async-start | bytes 2359296 | tf_op jit(solution)/shard_map/all_gather | solution.py:15
  85.9 251.4 %copy-start.1 = (f32[128,512]{1,0:T(8,128)S(1)}, f32[128,512]{1,0:T(8,128)}, u32[]{:S(2)}) copy-start(f32[128,512]{1,0:T(8,128)} %param.12) | copy-start | bytes 786436
  85.9 251.4 %copy-start.2 = (f32[1,128,512]{2,1,0:T(8,128)S(1)}, f32[1,128,512]{2,1,0:T(8,128)}, u32[]{:S(2)}) copy-start(f32[1,128,512]{2,1,0:T(8,128)} %param.9) | copy-start | bytes 786436
  85.9 251.4 %copy-start.3 = (f32[1,128,512]{2,1,0:T(8,128)S(1)}, f32[1,128,512]{2,1,0:T(8,128)}, u32[]{:S(2)}) copy-start(f32[1,128,512]{2,1,0:T(8,128)} %param.11) | copy-start | bytes 786436
  85.9 251.4 %copy-start.4 = (f32[1,128,512]{2,1,0:T(8,128)S(1)}, f32[1,128,512]{2,1,0:T(8,128)}, u32[]{:S(2)}) copy-start(f32[1,128,512]{2,1,0:T(8,128)} %param.10) | copy-start | bytes 786436
  342.9 44.0 %copy-start.5 = (f32[128,512]{1,0:T(8,128)S(1)}, f32[128,512]{1,0:T(8,128)}, u32[]{:S(2)}) copy-start(f32[128,512]{1,0:T(8,128)} %param.13) | copy-start | bytes 786436
  342.9 360.1 %copy-start = (bf16[1,128,8192]{2,1,0:T(8,128)(2,1)S(1)}, bf16[1,128,8192]{2,1,0:T(8,128)(2,1)}, u32[]{:S(2)}) copy-start(bf16[1,128,8192]{2,1,0:T(8,128)(2,1)} %param.7) | copy-start | bytes 6291460
  342.9 360.0 %all-gather.6.cloned.1.call-start = ((), (), s32[]{:S(2)}) async-start(), calls=%async_computation.1 | async-start | bytes 8519680 | tf_op jit(solution)/shard_map/all_gather | solution.py:45
Sparse Core Ops, SparseCore 0:
  10.1 327.0 all-gather.7
  343.0 41.9 all-gather.9
  387.8 315.1 all-gather.5

commit v2 on v0

--- a/solution.py
+++ b/solution.py
@@ -35,10 +35,17 @@
     summed_drift = lax.psum(drift, "rep")
     weights_next = outer_update(summed_drift / rep_count, anchor, outer_momentum)
     columns = tokens_local
+
+    def mark_the_sheet(local, peer_axis, on_dim):
+        return jnp.concatenate(
+            lax.all_to_all(
+                jnp.stack([local for _ in range(lax.axis_size(peer_axis))]), peer_axis, 0, 0
+            ),
+            axis=on_dim,
+        )
+
     values = jnp.dot(
-        columns,
-        lax.all_gather(weights_next, "fsdp", axis=0, tiled=True),
-        preferred_element_type=jnp.float32,
+        columns, mark_the_sheet(weights_next, "fsdp", 0), preferred_element_type=jnp.float32
     )
     return (first_next[None], values.astype(jnp.bfloat16)[None])
 

time: 756 us -> 633 us (0.84)
  the two profiles are of different devices: /device:TPU:2 before, /device:TPU:8 now
where the time goes in v2:
time: 633 us
  waiting for transfers between devices  329 us (52%)
  blocking collectives  272 us (43%)
  between operations  14.1 us (2%)
  local copies, waits for them, and re-layouts  8.34 us (1%)
  matrix products  8.06 us (1%)
    all_gather x1, waiting for transfers between devices, on_device(): lax.all_gather(cots_local, 'fsdp', axis=0, tiled=True)  239 us
    all_to_all x1, blocking collectives, mark_the_sheet(): lax.all_to_all(jnp.stack([local for _ in range(lax.axis_size(peer_axis))]...  195 us
    psum x1, waiting for transfers between devices, on_device(): summed_drift = lax.psum(drift, 'rep')  89.4 us
    all_to_all x1, blocking collectives, on_device(): lax.all_to_all(tokens_local, 'fsdp', split_axis=1, concat_axis=0, tiled=T...  77 us
  transfers between devices with their start and end apart: 2, of which 2 were waited for; matrix products, arithmetic and copies ran while one was open for 1% of the time, Pallas kernels for 0%

profile of v2, /device:TPU:8, one launch (start us, length us, event | category | flops | bytes accessed | tf_op | source)
XLA Modules:
  0.0 633.1 jit_solution(15325450039208415853)
XLA Ops:
  7.2 0.0 all-gather.3.cloned.1.call-start
  7.2 0.7 all-gather.3.cloned.1.call-update
  7.9 0.0 all-reduce.2.cloned.1.call-start
  7.9 3.2 copy.11
  11.2 77.0 %all_to_all.24 = bf16[128,64,128]{0,2,1:T(8,128)(2,1)} all-to-all(bf16[128,64,128]{0,2,1:T(8,128)(2,1)S(1)} %bitcast.37), channel_id=1, replica_groups=mesh['rep'=8,'fsdp'=64] {'fsdp'}, dimensions={1} | all-to-all | bytes 4194304 | tf_op jit(solution)/shard_map/all_to_all | solution.py:23
  88.2 0.0 copy-start.1
  88.2 0.0 copy-start.2
  88.2 0.0 copy-start.3
  88.2 0.0 copy-start.4
  88.2 3.3 copy.12
  91.5 239.2 %all-gather.3.cloned.1.call-done = bf16[1,8192,512]{2,1,0:T(8,128)(2,1)} async-done(((bf16[1,128,512]{2,1,0:T(8,128)(2,1)}), bf16[1,8192,512]{2,1,0:T(8,128)(2,1)}) %all-gather.3.cloned.1.call-update) | async-done | bytes 8388624 | tf_op jit(solution)/shard_map/all_gather | solution.py:27
  330.7 0.0 copy-done.1
  330.7 0.0 copy-done.2
  330.7 0.0 copy-done.3
  330.7 0.0 copy-done.4
  330.7 0.0 copy-start.5
  330.7 5.7 fusion.15
  336.4 0.0 all-reduce.2.cloned.1.call-update
  336.4 89.4 %all-reduce.2.cloned.1.call-done = f32[128,512]{1,0:T(8,128)} async-done(((f32[128,512]{1,0:T(8,128)}), f32[128,512]{1,0:T(8,128)}) %all-reduce.2.cloned.1.call-update) | async-done | bytes 262160 | tf_op jit(solution)/shard_map/psum | solution.py:35
  425.8 0.0 copy-done.5
  425.8 1.0 subtract_convert_fusion
  426.8 1.0 stack.2
  427.8 0.0 copy-start
  427.9 195.3 %all_to_all.25 = bf16[64,128,512]{2,1,0:T(8,128)(2,1)S(1)} all-to-all(bf16[64,128,512]{2,1,0:T(8,128)(2,1)S(1)} %stack.2), channel_id=1, replica_groups=mesh['rep'=8,'fsdp'=64] {'fsdp'}, dimensions={0} | all-to-all | bytes 16777216 | tf_op jit(solution)/shard_map/all_to_all | solution.py:41
  623.1 0.0 copy-done
  623.1 2.4 fusion.7
  625.5 0.8 copy.13
Async XLA Ops:
  7.2 323.5 %all-gather.3.cloned.1.call-start = ((), (), s32[]{:S(2)}) async-start(), calls=%async_computation.3 | async-start | bytes 8519680 | tf_op jit(solution)/shard_map/all_gather | solution.py:27
  7.9 417.9 %all-reduce.2.cloned.1.call-start = ((), (), s32[]{:S(2)}) async-start(), calls=%async_computation.2 | async-start | bytes 524288 | tf_op jit(solution)/shard_map/psum | solution.py:35
  88.2 242.5 %copy-start.1 = (f32[128,512]{1,0:T(8,128)S(1)}, f32[128,512]{1,0:T(8,128)}, u32[]{:S(2)}) copy-start(f32[128,512]{1,0:T(8,128)} %param.12) | copy-start | bytes 786436
  88.2 242.5 %copy-start.2 = (f32[1,128,512]{2,1,0:T(8,128)S(1)}, f32[1,128,512]{2,1,0:T(8,128)}, u32[]{:S(2)}) copy-start(f32[1,128,512]{2,1,0:T(8,128)} %param.9) | copy-start | bytes 786436
  88.2 242.5 %copy-start.3 = (f32[1,128,512]{2,1,0:T(8,128)S(1)}, f32[1,128,512]{2,1,0:T(8,128)}, u32[]{:S(2)}) copy-start(f32[1,128,512]{2,1,0:T(8,128)} %param.11) | copy-start | bytes 786436
  88.2 242.5 %copy-start.4 = (f32[1,128,512]{2,1,0:T(8,128)S(1)}, f32[1,128,512]{2,1,0:T(8,128)}, u32[]{:S(2)}) copy-start(f32[1,128,512]{2,1,0:T(8,128)} %param.10) | copy-start | bytes 786436
  330.7 95.1 %copy-start.5 = (f32[128,512]{1,0:T(8,128)S(1)}, f32[128,512]{1,0:T(8,128)}, u32[]{:S(2)}) copy-start(f32[128,512]{1,0:T(8,128)} %param.13) | copy-start | bytes 786436
  427.8 195.3 %copy-start = (bf16[1,128,8192]{2,1,0:T(8,128)(2,1)S(1)}, bf16[1,128,8192]{2,1,0:T(8,128)(2,1)}, u32[]{:S(2)}) copy-start(bf16[1,128,8192]{2,1,0:T(8,128)(2,1)} %param.7) | copy-start | bytes 6291460
Sparse Core Ops, SparseCore 0:
  10.1 320.5 all-gather.2
  336.6 89.1 all-reduce.1
